TPU v7x, 32 devices: a whole 2x2x4 slice. The times are simulated.
32 devices in a mesh: groups: 2 (over y), seq: 4 (over z), mp: 4 (over x, core).
Axes of the slice: x: 2, y: 2, z: 4, core: 2. Of those that a mesh axis runs over, the one named last changes fastest.
Arguments:
- node_vectors: bfloat16 [1024, 2048], P(('groups', 'seq'), 'mp'), parts along dimension 0, may hold values from -6 to 6
- standardize_multiplier: float32 [2048], replicated, may hold values from 0.1 to 1.9
- probe_matrix: bfloat16 [2048, 1024], P(None, 'mp'), may hold values from -1 to 1
- lookup_matrix: bfloat16 [2048, 1024], P(None, 'mp'), may hold values from -1 to 1
- content_matrix: bfloat16 [2048, 1024], P(None, 'mp'), may hold values from -0.125 to 0.125
- softness_per_group: float32 [8], P('mp'), may hold values from 0.5 to 12
- exit_matrix: bfloat16 [1024, 2048], P('mp'), may hold values from -0.1875 to 0.1875
Outputs:
- mixed: bfloat16 [1024, 2048], P(('groups', 'seq'), 'mp'), parts along dimension 0
There are 2 independent parts, one for each index of `groups`. A program takes and returns all parts, laid end to end along the dimension named above; an argument that names none is the same for every part. Nothing has to cross between parts.
All inputs are finite; a program needn't handle non-finite values.
Results may differ from a plain program's by a relative error of at most 0.011.
Values may be sent and summed in bfloat16 or wider, within the bound.
A program may use at most 64 MiB of HBM per device.

v0:
```python
import math
import jax
import jax.numpy as jnp
from jax import lax
from jax.sharding import PartitionSpec as P


def attend(state_in, blocks, query_heads, inverse_root_span, resident_groups, channel_span):
    running_max, running_sum, weighted = state_in
    key_block, value_block = blocks
    count = key_block.shape[0]
    key_heads = key_block.reshape(count, resident_groups, channel_span)
    value_heads = value_block.reshape(count, resident_groups, channel_span)
    scores = (
        jnp.einsum("rhd,nhd->hrn", query_heads, key_heads, preferred_element_type=jnp.float32)
        * inverse_root_span[:, None, None]
    )
    new_max = jnp.max(scores, axis=-1)
    rescale = jnp.exp(running_max - new_max)
    weights = jnp.exp(scores - new_max[:, :, None])
    running_sum = running_sum * rescale + jnp.sum(weights, axis=-1)
    update = jnp.einsum(
        "hrn,nhd->hrd",
        weights.astype(jnp.bfloat16),
        value_heads,
        preferred_element_type=jnp.float32,
    )
    weighted = weighted * rescale[:, :, None] + update
    return (new_max, running_sum, weighted)


def per_device(
    node_vectors,
    standardize_multiplier,
    probe_matrix,
    lookup_matrix,
    content_matrix,
    softness_per_group,
    exit_matrix,
):
    full_rows = lax.all_gather(node_vectors, "mp", axis=1, tiled=True)
    widened = full_rows.astype(jnp.float32)
    average = jnp.mean(widened, axis=-1, keepdims=True)
    centered = widened - average
    variance = jnp.mean(centered * centered, axis=-1, keepdims=True)
    normed = (centered * lax.rsqrt(variance + 1e-05) * standardize_multiplier).astype(jnp.bfloat16)
    queries = jnp.dot(normed, probe_matrix, preferred_element_type=jnp.float32).astype(jnp.bfloat16)
    key_rows = jnp.dot(normed, lookup_matrix, preferred_element_type=jnp.float32).astype(
        jnp.bfloat16
    )
    value_rows = jnp.dot(normed, content_matrix, preferred_element_type=jnp.float32).astype(
        jnp.bfloat16
    )
    resident_groups = softness_per_group.shape[0]
    head_cols = queries.shape[1]
    channel_span = head_cols // resident_groups
    token_count = queries.shape[0]
    query_heads = queries.reshape(token_count, resident_groups, channel_span)
    inverse_root_span = softness_per_group / math.sqrt(channel_span)
    initial = (
        jnp.full((resident_groups, token_count), -jnp.inf, jnp.float32),
        jnp.zeros((resident_groups, token_count), jnp.float32),
        jnp.zeros((resident_groups, token_count, channel_span), jnp.float32),
    )
    final = attend(
        initial,
        (
            lax.all_gather(key_rows, "seq", axis=0, tiled=True),
            lax.all_gather(value_rows, "seq", axis=0, tiled=True),
        ),
        query_heads,
        inverse_root_span,
        resident_groups,
        channel_span,
    )
    heads_out = (
        (final[2] / final[1][:, :, None])
        .transpose(1, 0, 2)
        .reshape(token_count, head_cols)
        .astype(jnp.bfloat16)
    )
    partial_sums = jnp.dot(heads_out, exit_matrix, preferred_element_type=jnp.float32)
    summed = lax.psum_scatter(
        partial_sums.astype(jnp.bfloat16), "mp", scatter_dimension=1, tiled=True
    ).astype(jnp.float32)
    return (node_vectors.astype(jnp.float32) + summed).astype(jnp.bfloat16)


def solution(mesh):
    return jax.shard_map(
        per_device,
        mesh=mesh,
        in_specs=(
            P(("groups", "seq"), "mp"),
            P(),
            P(None, "mp"),
            P(None, "mp"),
            P(None, "mp"),
            P("mp"),
            P("mp", None),
        ),
        out_specs=P(("groups", "seq"), "mp"),
        check_vma=False,
    )
```

profile of v0, /device:TPU:0, one launch (start us, length us, event | category | flops | bytes accessed | tf_op | source)
XLA Modules:
  0.0 81.6 jit_solution(14585379958456140718)
XLA Ops:
  6.5 0.0 copy-start
  6.5 0.0 copy-start.2
  6.5 0.0 reduce-scatter.2.cloned.1.call-start
  6.5 0.8 broadcast_multiply_fusion
  7.3 8.8 %all_gather.9 = bf16[128,2048]{1,0:T(8,128)(2,1)S(1)} all-gather(bf16[128,512]{1,0:T(8,128)(2,1)} %param.7), channel_id=1, replica_groups=mesh['groups'=2,'seq'=4,'mp'=4] {'mp'}, dimensions={1}, use_global_device_ids=true | all-gather | bytes 655360 | tf_op jit(solution)/shard_map/all_gather | solution.py:41
  16.2 0.2 convert_reduce_fusion
  16.4 0.0 copy-start.5
  16.4 0.3 fusion.6
  16.7 0.0 copy-done.2
  16.7 0.4 copy-done.5
  17.1 0.0 copy-start.3
  17.1 0.4 convolution_convert_fusion.2
  17.4 0.9 %copy-done.3 = bf16[2048,256]{1,0:T(8,128)(2,1)S(1)} copy-done((bf16[2048,256]{1,0:T(8,128)(2,1)S(1)}, bf16[2048,256]{1,0:T(8,128)(2,1)}, u32[]{:S(2)}) %copy-start.3) | copy-done | bytes 1048600
  18.3 0.0 copy-start.4
  18.3 0.4 convolution_convert_fusion.1
  18.6 0.9 %copy-done.4 = bf16[2048,256]{1,0:T(8,128)(2,1)S(1)} copy-done((bf16[2048,256]{1,0:T(8,128)(2,1)S(1)}, bf16[2048,256]{1,0:T(8,128)(2,1)}, u32[]{:S(2)}) %copy-start.4) | copy-done | bytes 1048600
  19.5 0.4 fusion.5
  19.9 14.1 %all_gather.11 = bf16[512,256]{1,0:T(8,128)(2,1)S(1)} all-gather(bf16[128,256]{1,0:T(8,128)(2,1)S(1)} %convolution_convert_fusion.1), channel_id=1, replica_groups=mesh['groups'=2,'seq'=4,'mp'=4] {'seq'}, dimensions={0}, use_global_device_ids=true | all-gather | bytes 327680 | tf_op jit(solution)/shard_map/all_gather | solution.py:69
  34.0 0.1 copy.11
  34.1 14.6 %all_gather.10 = bf16[512,256]{1,0:T(8,128)(2,1)S(1)} all-gather(bf16[128,256]{1,0:T(8,128)(2,1)S(1)} %convolution_convert_fusion.2), channel_id=1, replica_groups=mesh['groups'=2,'seq'=4,'mp'=4] {'seq'}, dimensions={0}, use_global_device_ids=true | all-gather | bytes 327680 | tf_op jit(solution)/shard_map/all_gather | solution.py:68
  48.7 0.3 fusion.20
  49.1 0.2 fusion.9
  49.3 0.3 fusion.4
  49.6 0.0 copy-done
  49.6 1.1 %convolution_convert_fusion = bf16[128,2048]{1,0:T(8,128)(2,1)} fusion(bf16[128,256]{0,1:T(8,128)(2,1)S(1)} %bitcast.39, bf16[256,2048]{1,0:T(8,128)(2,1)S(1)} %copy-done), kind=kOutput, calls=%fused_computation | convolution fusion | flops 134479872 | bytes 1638400 | tf_op jit(solution)/shard_map/dot_general | solution.py:82
  50.8 0.0 copy-start.1
  50.8 0.0 reduce-scatter.2.cloned.1.call-update
  50.8 22.4 %reduce-scatter.2.cloned.1.call-done = bf16[128,512]{1,0:T(8,128)(2,1)} async-done(((bf16[128,2048]{1,0:T(8,128)(2,1)}), bf16[128,512]{1,0:T(8,128)(2,1)}) %reduce-scatter.2.cloned.1.call-update) | async-done | bytes 131088 | tf_op jit(solution)/shard_map/reduce_scatter | solution.py:83
  73.2 0.0 copy-done.1
  73.2 1.6 %add_convert_fusion = bf16[128,512]{1,0:T(8,128)(2,1)} fusion(bf16[128,512]{1,0:T(8,128)(2,1)} %reduce-scatter.2.cloned.1.call-done, bf16[128,512]{1,0:T(8,128)(2,1)S(1)} %copy-done.1), kind=kLoop, calls=%fused_computation.22 | loop fusion | flops 262144 | bytes 393216 | tf_op jit(solution)/shard_map/convert_element_type | solution.py:86
  (4 shorter events, 0.0 us)
Async XLA Ops:
  6.5 43.1 %copy-start = (bf16[256,2048]{1,0:T(8,128)(2,1)S(1)}, bf16[256,2048]{1,0:T(8,128)(2,1)}, u32[]{:S(2)}) copy-start(bf16[256,2048]{1,0:T(8,128)(2,1)} %param.13) | copy-start | bytes 3145732
  6.5 10.1 %copy-start.2 = (bf16[2048,256]{1,0:T(8,128)(2,1)S(1)}, bf16[2048,256]{1,0:T(8,128)(2,1)}, u32[]{:S(2)}) copy-start(bf16[2048,256]{1,0:T(8,128)(2,1)} %param.10) | copy-start | bytes 3145732
  6.5 66.6 %reduce-scatter.2.cloned.1.call-start = ((), (), s32[]{:S(2)}) async-start(), calls=%async_computation.1 | async-start | bytes 655360 | tf_op jit(solution)/shard_map/reduce_scatter | solution.py:83
  16.4 0.7 copy-start.5
  17.1 1.2 %copy-start.3 = (bf16[2048,256]{1,0:T(8,128)(2,1)S(1)}, bf16[2048,256]{1,0:T(8,128)(2,1)}, u32[]{:S(2)}) copy-start(bf16[2048,256]{1,0:T(8,128)(2,1)} %param.11) | copy-start | bytes 3145732
  18.3 1.2 %copy-start.4 = (bf16[2048,256]{1,0:T(8,128)(2,1)S(1)}, bf16[2048,256]{1,0:T(8,128)(2,1)}, u32[]{:S(2)}) copy-start(bf16[2048,256]{1,0:T(8,128)(2,1)} %param.9) | copy-start | bytes 3145732
  50.8 22.4 %copy-start.1 = (bf16[128,512]{1,0:T(8,128)(2,1)S(1)}, bf16[128,512]{1,0:T(8,128)(2,1)}, u32[]{:S(2)}) copy-start(bf16[128,512]{1,0:T(8,128)(2,1)} %param.7) | copy-start | bytes 393220
Sparse Core Ops, SparseCore 0:
  50.9 22.2 reduce-scatter.1
where the time goes:
time: 81.9 us; the launch traced here: 81.6 us
  blocking collectives  37.6 us (46%)
  waiting for transfers between devices  22.4 us (27%)
  between operations  13.5 us (16%)
  other arithmetic  3.1 us (4%)
  matrix products  2.85 us (3%)
  local copies, waits for them, and re-layouts  2.25 us (3%)
    reduce_scatter x1, waiting for transfers between devices, per_device(): lax.psum_scatter(partial_sums.astype(jnp.bfloat16), 'mp', scatter_dimensi...  22.4 us
    all_gather x1, blocking collectives, per_device(): lax.all_gather(key_rows, 'seq', axis=0, tiled=True)  14.6 us
    all_gather x1, blocking collectives, per_device(): lax.all_gather(value_rows, 'seq', axis=0, tiled=True)  14.1 us
    all_gather x1, blocking collectives, per_device(): full_rows = lax.all_gather(node_vectors, 'mp', axis=1, tiled=True)  8.84 us
    unnamed x12, local copies, waits for them, and re-layouts  2.11 us
  transfers between devices with their start and end apart: 1, of which 1 were waited for; matrix products, arithmetic and copies ran while one was open for 0% of the time, Pallas kernels for 0%

commit v1 on v0

--- a/solution.py
+++ b/solution.py
@@ -62,12 +62,21 @@
         jnp.zeros((resident_groups, token_count), jnp.float32),
         jnp.zeros((resident_groups, token_count, channel_span), jnp.float32),
     )
+
+    def supply_all_the_chains(mat, array_dim=0):
+        x_now, moved = (lax.axis_size("seq"), lax.axis_index("seq"))
+        d_next, state_next = (mat, 1)
+        while state_next < x_now:
+            u_next = lax.ppermute(d_next, "seq", [(t, t ^ state_next) for t in range(x_now)])
+            b_next = jnp.concatenate([d_next, u_next], array_dim)
+            val = jnp.concatenate([u_next, d_next], array_dim)
+            d_next = jnp.where(moved & state_next == 0, b_next, val)
+            state_next = 2 * state_next
+        return d_next
+
     final = attend(
         initial,
-        (
-            lax.all_gather(key_rows, "seq", axis=0, tiled=True),
-            lax.all_gather(value_rows, "seq", axis=0, tiled=True),
-        ),
+        (supply_all_the_chains(key_rows), lax.all_gather(value_rows, "seq", axis=0, tiled=True)),
         query_heads,
         inverse_root_span,
         resident_groups,

time: 81.9 us -> 74 us (0.904)
  blocking collectives: 37.6 us -> 23 us
  waiting for transfers between devices: 22.4 us -> 27.2 us
  starting transfers between devices: 0.01 us -> 2.36 us
  matrix products: 2.85 us -> 4.17 us
  local copies, waits for them, and re-layouts: 2.25 us -> 1.21 us
    all_gather x1 -> x0, blocking collectives: 14.6 us -> none  [per_device(): lax.all_gather(key_rows, 'seq', axis=0, tiled=True)]
    ppermute x0 -> x2, waiting for transfers between devices: none -> 6.54 us  [supply_all_the_chains(): lax.ppermute(d_next, 'seq', [(t, t ^ state_next) for t in range(x_now)])]
    ppermute x0 -> x2, starting transfers between devices: none -> 2.36 us  [supply_all_the_chains(): lax.ppermute(d_next, 'seq', [(t, t ^ state_next) for t in range(x_now)])]
    reduce_scatter x1, waiting for transfers between devices: 22.4 us -> 20.7 us  [per_device(): lax.psum_scatter(partial_sums.astype(jnp.bfloat16), 'mp', scatter_dimensi...]
    dot_general x1, matrix products: 0.36 us -> 1.67 us  [per_device(): jnp.dot(normed, content_matrix, preferred_element_type=jnp.float32)]
    unnamed x12, local copies, waits for them, and re-layouts: 2.11 us -> 1.05 us
  transfers between devices with their start and end apart: 1 -> 3, of which waited for: 1 -> 2; matrix products, arithmetic and copies ran while one was open for 0% -> 3% of each run, Pallas kernels for 0% -> 0%
where the time goes in v1:
time: 74 us; the launch traced here: 73.8 us
  waiting for transfers between devices  27.2 us (37%)
  blocking collectives  23 us (31%)
  between operations  13.5 us (18%)
  matrix products  4.17 us (6%)
  other arithmetic  2.37 us (3%)
  starting transfers between devices  2.36 us (3%)
  local copies, waits for them, and re-layouts  1.21 us (2%)
    reduce_scatter x1, waiting for transfers between devices, per_device(): lax.psum_scatter(partial_sums.astype(jnp.bfloat16), 'mp', scatter_dimensi...  20.7 us
    all_gather x1, blocking collectives, per_device(): lax.all_gather(value_rows, 'seq', axis=0, tiled=True)  14 us
    all_gather x1, blocking collectives, per_device(): full_rows = lax.all_gather(node_vectors, 'mp', axis=1, tiled=True)  8.97 us
    ppermute x2, waiting for transfers between devices, supply_all_the_chains(): lax.ppermute(d_next, 'seq', [(t, t ^ state_next) for t in range(x_now)])  6.54 us
    ppermute x2, starting transfers between devices, supply_all_the_chains(): lax.ppermute(d_next, 'seq', [(t, t ^ state_next) for t in range(x_now)])  2.36 us
    dot_general x1, matrix products, per_device(): jnp.dot(normed, content_matrix, preferred_element_type=jnp.float32)  1.67 us
    convert_element_type x1, other arithmetic, per_device(): return (node_vectors.astype(jnp.float32) + summed).astype(jnp.bfloat16)  1.59 us
  transfers between devices with their start and end apart: 3, of which 2 were waited for; matrix products, arithmetic and copies ran while one was open for 3% of the time, Pallas kernels for 0%

profile of v1, /device:TPU:0, one launch (start us, length us, event | category | flops | bytes accessed | tf_op | source)
XLA Modules:
  0.0 73.8 jit_solution(7276348698729742428)
XLA Ops:
  6.5 0.0 copy-start
  6.5 0.0 copy-start.2
  6.5 0.0 reduce-scatter.2.cloned.1.call-start
  6.5 9.0 %all_gather.6 = bf16[128,2048]{1,0:T(8,128)(2,1)S(1)} all-gather(bf16[128,512]{1,0:T(8,128)(2,1)} %param.7), channel_id=1, replica_groups=mesh['groups'=2,'seq'=4,'mp'=4] {'mp'}, dimensions={1}, use_global_device_ids=true | all-gather | bytes 655360 | tf_op jit(solution)/shard_map/all_gather | solution.py:41
  15.5 0.2 convert_reduce_fusion
  15.7 0.0 copy-start.4
  15.7 0.3 fusion.6
  16.0 0.0 copy-done.2
  16.0 0.4 copy-done.4
  16.4 0.4 convolution_convert_fusion.2
  16.7 1.6 %collective-permute-start = (bf16[128,256]{1,0:T(8,128)(2,1)S(1)}, bf16[128,256]{1,0:T(8,128)(2,1)S(1)}, u32[]{:S(2)}, u32[]{:S(2)}) collective-permute-start(bf16[128,256]{1,0:T(8,128)(2,1)S(1)} %convolution_convert_fusion.2), channel_id=1, source_target_pairs={{0,4},{4,0},{8,12},{12,8},{1,5},{5,1},{9,13},{13,9},{2,6},{6,2},{1... | collective-permute-start | bytes 196616 | tf_op jit(solution)/shard_map/ppermute | solution.py:70
  18.4 0.0 copy-start.5
  18.4 0.6 copy-done.5
  19.1 0.0 copy-start.3
  19.1 1.7 %convolution_convert_fusion.1 = bf16[128,256]{1,0:T(8,128)(2,1)S(1)} fusion(bf16[2048,256]{1,0:T(8,128)(2,1)} %param.11, bf16[128,2048]{1,0:T(8,128)(2,1)S(1)} %all_gather.6, f32[2048]{0:T(1024)S(1)} %copy-done.4, f32[128]{0:T(128)S(1)} %add_rsqrt_fusion, f32[128]{0:T(128)S(1)} %broadcast_multiply_fusion.1), kind=kOutput, calls=%fused_computation.10 | convolution fusion | flops 135561216 | bytes 1647616 | tf_op jit(solution)/shard_map/dot_general | solution.py:51
  20.7 0.0 copy-done.3
  20.8 0.4 fusion.5
  21.1 14.0 %all_gather.7 = bf16[512,256]{1,0:T(8,128)(2,1)S(1)} all-gather(bf16[128,256]{1,0:T(8,128)(2,1)S(1)} %convolution_convert_fusion.1), channel_id=1, replica_groups=mesh['groups'=2,'seq'=4,'mp'=4] {'seq'}, dimensions={0}, use_global_device_ids=true | all-gather | bytes 327680 | tf_op jit(solution)/shard_map/all_gather | solution.py:79
  35.1 0.1 copy.16
  35.3 0.0 collective-permute-done
  35.3 0.7 collective-permute-start.1
  36.1 6.5 %collective-permute-done.1 = bf16[256,256]{1,0:T(8,128)(2,1)S(1)} collective-permute-done((bf16[256,256]{1,0:T(8,128)(2,1)S(1)}, bf16[256,256]{1,0:T(8,128)(2,1)S(1)}, u32[]{:S(2)}, u32[]{:S(2)}) %collective-permute-start.1) | collective-permute-done | bytes 131104 | tf_op jit(solution)/shard_map/ppermute | solution.py:70
  42.6 0.3 fusion.25
  43.0 0.2 fusion.9
  43.2 0.3 fusion.4
  43.5 0.0 copy-done
  43.6 1.1 %convolution_convert_fusion = bf16[128,2048]{1,0:T(8,128)(2,1)} fusion(bf16[128,256]{0,1:T(8,128)(2,1)S(1)} %bitcast.45, bf16[256,2048]{1,0:T(8,128)(2,1)S(1)} %copy-done), kind=kOutput, calls=%fused_computation | convolution fusion | flops 134479872 | bytes 1638400 | tf_op jit(solution)/shard_map/dot_general | solution.py:91
  44.7 0.0 copy-start.1
  44.7 0.0 reduce-scatter.2.cloned.1.call-update
  44.7 20.7 %reduce-scatter.2.cloned.1.call-done = bf16[128,512]{1,0:T(8,128)(2,1)} async-done(((bf16[128,2048]{1,0:T(8,128)(2,1)}), bf16[128,512]{1,0:T(8,128)(2,1)}) %reduce-scatter.2.cloned.1.call-update) | async-done | bytes 131088 | tf_op jit(solution)/shard_map/reduce_scatter | solution.py:92
  65.4 0.0 copy-done.1
  65.4 1.6 %add_convert_fusion = bf16[128,512]{1,0:T(8,128)(2,1)} fusion(bf16[128,512]{1,0:T(8,128)(2,1)} %reduce-scatter.2.cloned.1.call-done, bf16[128,512]{1,0:T(8,128)(2,1)S(1)} %copy-done.1), kind=kLoop, calls=%fused_computation.26 | loop fusion | flops 262144 | bytes 393216 | tf_op jit(solution)/shard_map/convert_element_type | solution.py:95
  (10 shorter events, 0.1 us)
Async XLA Ops:
  6.5 37.0 %copy-start = (bf16[256,2048]{1,0:T(8,128)(2,1)S(1)}, bf16[256,2048]{1,0:T(8,128)(2,1)}, u32[]{:S(2)}) copy-start(bf16[256,2048]{1,0:T(8,128)(2,1)} %param.13) | copy-start | bytes 3145732
  6.5 9.4 %copy-start.2 = (bf16[2048,256]{1,0:T(8,128)(2,1)S(1)}, bf16[2048,256]{1,0:T(8,128)(2,1)}, u32[]{:S(2)}) copy-start(bf16[2048,256]{1,0:T(8,128)(2,1)} %param.10) | copy-start | bytes 3145732
  6.5 58.8 %reduce-scatter.2.cloned.1.call-start = ((), (), s32[]{:S(2)}) async-start(), calls=%async_computation.1 | async-start | bytes 655360 | tf_op jit(solution)/shard_map/reduce_scatter | solution.py:92
  15.7 0.7 copy-start.4
  16.7 18.5 %collective-permute-start = (bf16[128,256]{1,0:T(8,128)(2,1)S(1)}, bf16[128,256]{1,0:T(8,128)(2,1)S(1)}, u32[]{:S(2)}, u32[]{:S(2)}) collective-permute-start(bf16[128,256]{1,0:T(8,128)(2,1)S(1)} %convolution_convert_fusion.2), channel_id=1, source_target_pairs={{0,4},{4,0},{8,12},{12,8},{1,5},{5,1},{9,13},{13,9},{2,6},{6,2},{1... | collective-permute-start | bytes 196616 | tf_op jit(solution)/shard_map/ppermute | solution.py:70
  18.4 0.7 copy-start.5
  19.1 1.7 %copy-start.3 = (bf16[2048,256]{1,0:T(8,128)(2,1)S(1)}, bf16[2048,256]{1,0:T(8,128)(2,1)}, u32[]{:S(2)}) copy-start(bf16[2048,256]{1,0:T(8,128)(2,1)} %param.9) | copy-start | bytes 3145732
  35.3 7.3 %collective-permute-start.1 = (bf16[256,256]{1,0:T(8,128)(2,1)S(1)}, bf16[256,256]{1,0:T(8,128)(2,1)S(1)}, u32[]{:S(2)}, u32[]{:S(2)}) collective-permute-start(bf16[256,256]{1,0:T(8,128)(2,1)S(1)} %maximum_select_fusion.3), channel_id=1, source_target_pairs={{0,8},{4,12},{8,0},{12,4},{1,9},{5,13},{9,1},{13,5},{2,10},{6,14},... | collective-permute-start | bytes 393224 | tf_op jit(solution)/shard_map/ppermute | solution.py:70
  44.7 20.7 %copy-start.1 = (bf16[128,512]{1,0:T(8,128)(2,1)S(1)}, bf16[128,512]{1,0:T(8,128)(2,1)}, u32[]{:S(2)}) copy-start(bf16[128,512]{1,0:T(8,128)(2,1)} %param.7) | copy-start | bytes 393220
Sparse Core Ops, SparseCore 0:
  44.8 20.4 reduce-scatter.1
